TPU v7x, 32 devices: a whole 2x2x4 slice. The times are simulated.
32 devices in a mesh: row: 8 (over y, x, core), col: 4 (over z).
Axes of the slice: x: 2, y: 2, z: 4, core: 2. Of those that a mesh axis runs over, the one named last changes fastest.
Arguments:
- alignment: float32 [192, 16, 64], P('row', 'col'), may hold values from -6 to 6
- pair_state: float32 [192, 192, 128], P('row', 'col'), may hold values from -6 to 6
- pair_weights: float32 [8, 192, 192], P(None, 'row', 'col'), may hold values from 0 to 1, as said below
- align_gain: float32 [64], replicated, may hold values from 0.5 to 2
- value_weight: float32 [64, 256], replicated, may hold values from -0.75 to 0.75
- gate_weight: float32 [64, 256], replicated, may hold values from -0.75 to 0.75
- output_weight: float32 [256, 64], replicated, may hold values from -0.375 to 0.375
- outer_gain: float32 [64], replicated, may hold values from 0.5 to 2
- left_weight: float32 [64, 32], replicated, may hold values from -0.75 to 0.75
- right_weight: float32 [64, 32], replicated, may hold values from -0.75 to 0.75
- outer_weight: float32 [1024, 128], replicated, may hold values from -0.75 to 0.75
- outer_bias: float32 [128], replicated, may hold values from -3 to 3
Outputs:
- alignment_out: float32 [192, 16, 64], P('row', 'col')
- pair_out: float32 [192, 192, 128], P('row', 'col')
Inputs may be any that keep to these rules, and one draw needn't show every extreme that they name: `pair_weights`: every entry is positive, and for each head and row token the weights over the 192 column tokens sum to one.
All inputs are finite; a program needn't handle non-finite values.
Results may differ from a plain program's by a relative error of at most 0.00011.
Values sent between devices are 32-bit elements; how exact they have to be, the bound alone decides.
A program may use at most 64 MiB of HBM per device.

v0:
```python
import jax
import jax.numpy as jnp
from jax import lax
from jax.sharding import PartitionSpec as P

PRECISE = lax.Precision.HIGHEST


def normalize(features, channel_gain):
    channel_mean = jnp.mean(features, axis=-1, keepdims=True)
    centered = features - channel_mean
    spread = jnp.mean(centered * centered, axis=-1, keepdims=True)
    return centered * lax.rsqrt(spread + 1e-05) * channel_gain


def on_device(
    alignment,
    pair_state,
    pair_weights,
    align_gain,
    value_weight,
    gate_weight,
    output_weight,
    outer_gain,
    left_weight,
    right_weight,
    outer_weight,
    outer_bias,
):
    head_count = pair_weights.shape[0]
    local_rows = alignment.shape[0]
    local_seqs = alignment.shape[1]
    channels = alignment.shape[2]
    normed = normalize(alignment, align_gain)
    flat_normed = normed.reshape(local_rows, local_seqs * channels)
    gathered = lax.all_gather(flat_normed, "row", axis=0, tiled=True)
    gathered = gathered.reshape(-1, local_seqs, channels)
    mixed_rows = jnp.einsum(
        "hij,jsc->ishc",
        lax.all_gather(pair_weights, "col", axis=2, tiled=True),
        gathered,
        precision=PRECISE,
    )
    per_head = value_weight.reshape(channels, head_count, -1)
    averaged = jnp.einsum("ishc,chd->ishd", mixed_rows, per_head, precision=PRECISE)
    gate_values = jax.nn.sigmoid(jnp.einsum("nsc,cd->nsd", normed, gate_weight, precision=PRECISE))
    gated_heads = gate_values * averaged.reshape(gate_values.shape)
    alignment_out = alignment + jnp.einsum(
        "nsd,dc->nsc", gated_heads, output_weight, precision=PRECISE
    )
    normed_out = normalize(alignment_out, outer_gain)
    left_side = jnp.einsum("nsc,cd->nsd", normed_out, left_weight, precision=PRECISE)
    right_side = jnp.einsum("nsc,cd->nsd", normed_out, right_weight, precision=PRECISE)
    factor_width = left_side.shape[2]
    columns = pair_state.shape[1]
    left_flat = left_side.transpose(1, 0, 2).reshape(local_seqs, local_rows * factor_width)
    right_rows = right_side.reshape(local_rows, local_seqs * factor_width)
    right_tokens = lax.all_gather(right_rows, "row", axis=0, tiled=True)
    right_tokens = right_tokens.reshape(-1, local_seqs, factor_width)
    right_columns = lax.all_to_all(right_tokens, "col", split_axis=0, concat_axis=1, tiled=True)
    right_all = right_columns.transpose(1, 0, 2)
    left_all = lax.all_gather(left_flat, "col", axis=0, tiled=True)
    sequences = left_all.shape[0]
    left_all = left_all.reshape(sequences, local_rows, factor_width)
    block_rows = 8
    left_blocks = left_all.reshape(
        sequences, local_rows // block_rows, block_rows, factor_width
    ).transpose(1, 2, 0, 3)

    def outer_block(left_block):
        product = jnp.einsum("isc,sjd->ijcd", left_block, right_all, precision=PRECISE) / sequences
        flattened = product.reshape(-1, factor_width * factor_width)
        projected = jnp.dot(
            flattened, outer_weight, precision=PRECISE, preferred_element_type=jnp.float32
        )
        return projected.reshape(block_rows, columns, -1)

    update = lax.map(outer_block, left_blocks).reshape(pair_state.shape)
    pair_out = pair_state + update + outer_bias
    return (alignment_out, pair_out)


def solution(mesh):
    return jax.shard_map(
        on_device,
        mesh=mesh,
        in_specs=(
            P("row", "col", None),
            P("row", "col", None),
            P(None, "row", "col"),
            P(),
            P(),
            P(),
            P(),
            P(),
            P(),
            P(),
            P(),
            P(),
        ),
        out_specs=(P("row", "col", None), P("row", "col", None)),
        check_vma=False,
    )
```

profile of v0, /device:TPU:0, one launch (start us, length us, event | category | flops | bytes accessed | tf_op | source)
XLA Modules:
  0.0 132.7 jit_solution(414286124162708641)
XLA Ops:
  0.7 1.0 reduce_sum.36
  1.7 1.0 multiply_reduce_fusion.1
  3.7 10.9 %all_gather.12 = f32[192,256]{1,0:T(8,128)S(1)} all-gather(f32[24,256]{1,0:T(8,128)S(1)} %reshape.65), channel_id=1, replica_groups=mesh['row'=8,'col'=4] {'row'}, dimensions={0}, use_global_device_ids=true | all-gather | bytes 221184 | tf_op jit(solution)/shard_map/all_gather | solution.py:36
  14.7 1.0 copy.89
  15.7 19.8 %all_gather.13 = f32[8,24,192]{1,0,2:T(8,128)S(1)} all-gather(f32[8,24,48]{1,0,2:T(8,128)S(1)} %copy.89), channel_id=1, replica_groups=mesh['row'=8,'col'=4] {'col'}, dimensions={2}, use_global_device_ids=true | all-gather | bytes 184320 | tf_op jit(solution)/shard_map/all_gather | solution.py:40
  35.5 0.9 copy.91
  36.5 1.5 %convolution_bitcast_fusion.2 = f32[24,4,8,64]{3,0,1,2:T(8,128)S(1)} fusion(f32[192,4,64,1]{0,2,1,3:T(8,128)S(1)} %bitcast.87, f32[8,24,192,1]{1,0,2,3:T(8,128)S(1)} %bitcast.83), kind=kOutput, calls=%fused_computation.8 | convolution fusion | flops 113246208 | bytes 540672 | tf_op jit(solution)/shard_map/hij,jsc->ishc/dot_general | solution.py:38
  40.0 9.2 %all_gather.15 = f32[192,128]{1,0:T(8,128)S(1)} all-gather(f32[24,128]{1,0:T(8,128)S(1)} %reshape.70), channel_id=1, replica_groups=mesh['row'=8,'col'=4] {'row'}, dimensions={0}, use_global_device_ids=true | all-gather | bytes 110592 | tf_op jit(solution)/shard_map/all_gather | solution.py:58
  50.5 3.3 %all-to-all-start = ((f32[4,1,6144]{2,1,0:T(1,128)}), f32[4,1,6144]{2,1,0:T(1,128)S(1)}, u32[]{:S(2)}, u32[]{:S(2)}) async-start(f32[4,1,6144]{2,1,0:T(1,128)} %reshape.87), calls=%async_computation | async-start | bytes 196608 | tf_op jit(solution)/shard_map/all_to_all | solution.py:60
  54.8 13.6 %all-gather = f32[4,4,768]{2,1,0:T(4,128)S(1)} all-gather(f32[1,4,768]{2,1,0:T(4,128)S(1)} %reshape.73), channel_id=1, replica_groups=mesh['row'=8,'col'=4] {'col'}, dimensions={0}, use_global_device_ids=true | all-gather | bytes 61440 | tf_op jit(solution)/shard_map/all_gather | solution.py:62
  70.6 60.2 %while.10 = (s32[]{:T(128)}, f32[3,8,48,128]{3,2,1,0:T(8,128)}, f32[3,8,16,32]{3,1,0,2:T(8,128)S(1)}, f32[16,48,32]{1,0,2:T(8,128)S(1)}, f32[1024,128]{1,0:T(8,128)S(1)}, /*index=5*/s32[]{:T(128)}) while((s32[]{:T(128)}, f32[3,8,48,128]{3,2,1,0:T(8,128)}, f32[3,8,16,32]{3,1,0,2:T(8,128)S(1)}, f32[16,48,32]{1,0,2:T(8,128)S(1)}, ...), condition=%wide.region_5.6_spmd, body=%wide.region_4.5_spmd.sunk | while | flops 679870464 | bytes 10306121 | solution.py:78
  70.6 5.1 %multiply_bitcast_fusion.2 = f32[8,48,32,32]{1,2,3,0:T(8,128)} fusion(f32[16,48,32]{1,0,2:T(8,128)S(1)} %get-tuple-element.125, f32[1,8,16,32]{3,1,0,2:T(8,128)S(1)} %constant_dynamic-slice_fusion.2), kind=kOutput, calls=%fused_computation.clone.1 | convolution fusion | flops 75890688 | bytes 1687552 | tf_op jit(solution)/shard_map/while/body/eval_jaxpr/isc,sjd->ijcd/dot_general | solution.py:71
  75.7 7.9 %copy.122 = f32[8,48,32,32]{3,2,1,0:T(8,128)} copy(f32[8,48,32,32]{1,2,3,0:T(8,128)} %multiply_bitcast_fusion.2) | data formatting | bytes 3145728 | tf_op jit(solution)/shard_map/while/body/eval_jaxpr/div | solution.py:71
  83.5 5.0 %reshape.90 = f32[8,48,1024]{2,1,0:T(8,128)S(1)} reshape(f32[8,48,32,32]{3,2,1,0:T(8,128)} %copy.122) | data formatting | bytes 3145728 | tf_op jit(solution)/shard_map/reshape.27
  88.6 2.1 %fusion.34 = f32[3,8,48,128]{3,2,1,0:T(8,128)} fusion(f32[3,8,48,128]{3,2,1,0:T(8,128)} %get-tuple-element.117, s32[]{:T(128)} %get-tuple-element.116, f32[8,48,1024]{2,1,0:T(8,128)S(1)} %reshape.90, f32[1024,128]{1,0:T(8,128)S(1)} %get-tuple-element.126), kind=kOutput, calls=%fused_computation.2.clone.1 | convolution fusion | flops 603979776 | bytes 2294272 | tf_op jit(solution)/shard_map/while/body/eval_jaxpr/dot_general | solution.py:73
  90.7 5.1 %multiply_bitcast_fusion.2 = f32[8,48,32,32]{1,2,3,0:T(8,128)} fusion(f32[16,48,32]{1,0,2:T(8,128)S(1)} %get-tuple-element.125, f32[1,8,16,32]{3,1,0,2:T(8,128)S(1)} %constant_dynamic-slice_fusion.2), kind=kOutput, calls=%fused_computation.clone.1 | convolution fusion | flops 75890688 | bytes 1687552 | tf_op jit(solution)/shard_map/while/body/eval_jaxpr/isc,sjd->ijcd/dot_general | solution.py:71
  95.7 7.9 %copy.122 = f32[8,48,32,32]{3,2,1,0:T(8,128)} copy(f32[8,48,32,32]{1,2,3,0:T(8,128)} %multiply_bitcast_fusion.2) | data formatting | bytes 3145728 | tf_op jit(solution)/shard_map/while/body/eval_jaxpr/div | solution.py:71
  103.6 5.0 %reshape.90 = f32[8,48,1024]{2,1,0:T(8,128)S(1)} reshape(f32[8,48,32,32]{3,2,1,0:T(8,128)} %copy.122) | data formatting | bytes 3145728 | tf_op jit(solution)/shard_map/reshape.27
  108.6 2.1 %fusion.34 = f32[3,8,48,128]{3,2,1,0:T(8,128)} fusion(f32[3,8,48,128]{3,2,1,0:T(8,128)} %get-tuple-element.117, s32[]{:T(128)} %get-tuple-element.116, f32[8,48,1024]{2,1,0:T(8,128)S(1)} %reshape.90, f32[1024,128]{1,0:T(8,128)S(1)} %get-tuple-element.126), kind=kOutput, calls=%fused_computation.2.clone.1 | convolution fusion | flops 603979776 | bytes 2294272 | tf_op jit(solution)/shard_map/while/body/eval_jaxpr/dot_general | solution.py:73
  110.7 5.1 %multiply_bitcast_fusion.2 = f32[8,48,32,32]{1,2,3,0:T(8,128)} fusion(f32[16,48,32]{1,0,2:T(8,128)S(1)} %get-tuple-element.125, f32[1,8,16,32]{3,1,0,2:T(8,128)S(1)} %constant_dynamic-slice_fusion.2), kind=kOutput, calls=%fused_computation.clone.1 | convolution fusion | flops 75890688 | bytes 1687552 | tf_op jit(solution)/shard_map/while/body/eval_jaxpr/isc,sjd->ijcd/dot_general | solution.py:71
  115.8 7.9 %copy.122 = f32[8,48,32,32]{3,2,1,0:T(8,128)} copy(f32[8,48,32,32]{1,2,3,0:T(8,128)} %multiply_bitcast_fusion.2) | data formatting | bytes 3145728 | tf_op jit(solution)/shard_map/while/body/eval_jaxpr/div | solution.py:71
  123.6 5.0 %reshape.90 = f32[8,48,1024]{2,1,0:T(8,128)S(1)} reshape(f32[8,48,32,32]{3,2,1,0:T(8,128)} %copy.122) | data formatting | bytes 3145728 | tf_op jit(solution)/shard_map/reshape.27
  128.7 2.1 %fusion.34 = f32[3,8,48,128]{3,2,1,0:T(8,128)} fusion(f32[3,8,48,128]{3,2,1,0:T(8,128)} %get-tuple-element.117, s32[]{:T(128)} %get-tuple-element.116, f32[8,48,1024]{2,1,0:T(8,128)S(1)} %reshape.90, f32[1024,128]{1,0:T(8,128)S(1)} %get-tuple-element.126), kind=kOutput, calls=%fused_computation.2.clone.1 | convolution fusion | flops 603979776 | bytes 2294272 | tf_op jit(solution)/shard_map/while/body/eval_jaxpr/dot_general | solution.py:73
  130.8 1.9 %fusion.8 = f32[24,48,128]{2,1,0:T(8,128)} fusion(f32[24,48,128]{2,1,0:T(8,128)S(1)} %copy-done.3, f32[3,8,48,128]{3,2,1,0:T(8,128)} %get-tuple-element.29, f32[128]{0:T(128)S(1)} %copy-done.5), kind=kLoop, calls=%fused_computation.18 | loop fusion | flops 294912 | bytes 1769984 | tf_op jit(solution)/shard_map/add | solution.py:79
  (51 shorter events, 7.4 us)
Async XLA Ops:
  0.6 38.3 %copy-start = (f32[64,256]{1,0:T(8,128)S(1)}, f32[64,256]{1,0:T(8,128)}, u32[]{:S(2)}) copy-start(f32[64,256]{1,0:T(8,128)} %param.19) | copy-start | bytes 196612
  0.6 38.5 %copy-start.2 = (f32[24,4,64]{2,1,0:T(4,128)S(1)}, f32[24,4,64]{2,1,0:T(4,128)}, u32[]{:S(2)}) copy-start(f32[24,4,64]{2,1,0:T(4,128)} %param.14) | copy-start | bytes 73732
  0.7 38.5 %copy-start.4 = (f32[256,64]{0,1:T(8,128)S(1)}, f32[256,64]{0,1:T(8,128)}, u32[]{:S(2)}) copy-start(f32[256,64]{0,1:T(8,128)} %param.20) | copy-start | bytes 196612
  0.7 39.0 %copy-start.8 = (f32[64]{0:T(128)S(1)}, f32[64]{0:T(128)}, u32[]{:S(2)}) copy-start(f32[64]{0:T(128)} %param.21) | copy-start | bytes 772
  0.7 39.0 %copy-start.6 = (f32[64,32]{0,1:T(8,128)S(1)}, f32[64,32]{0,1:T(8,128)}, u32[]{:S(2)}) copy-start(f32[64,32]{0,1:T(8,128)} %param.23) | copy-start | bytes 24580
  3.7 50.8 %copy-start.7 = (f32[64,32]{0,1:T(8,128)S(1)}, f32[64,32]{0,1:T(8,128)}, u32[]{:S(2)}) copy-start(f32[64,32]{0,1:T(8,128)} %param.22) | copy-start | bytes 24580
  36.5 34.1 %copy-start.1 = (f32[1024,128]{1,0:T(8,128)S(1)}, f32[1024,128]{1,0:T(8,128)}, u32[]{:S(2)}) copy-start(f32[1024,128]{1,0:T(8,128)} %param.24) | copy-start | bytes 1572868
  50.5 18.1 %all-to-all-start = ((f32[4,1,6144]{2,1,0:T(1,128)}), f32[4,1,6144]{2,1,0:T(1,128)S(1)}, u32[]{:S(2)}, u32[]{:S(2)}) async-start(f32[4,1,6144]{2,1,0:T(1,128)} %reshape.87), calls=%async_computation | async-start | bytes 196608 | tf_op jit(solution)/shard_map/all_to_all | solution.py:60
  70.5 60.2 %copy-start.3 = (f32[24,48,128]{2,1,0:T(8,128)S(1)}, f32[24,48,128]{2,1,0:T(8,128)}, u32[]{:S(2)}) copy-start(f32[24,48,128]{2,1,0:T(8,128)} %param.15) | copy-start | bytes 1769476
  70.5 60.2 %copy-start.5 = (f32[128]{0:T(128)S(1)}, f32[128]{0:T(128)}, u32[]{:S(2)}) copy-start(f32[128]{0:T(128)} %param.25) | copy-start | bytes 1540
where the time goes:
time: 134 us; the launch traced here: 133 us
  blocking collectives  53.6 us (40%)
  local copies, waits for them, and re-layouts  44.6 us (33%)
  matrix products  24.4 us (18%)
  other arithmetic  5.88 us (4%)
  starting transfers between devices  3.3 us (2%)
    div x3, local copies, waits for them, and re-layouts, outer_block(): jnp.einsum('isc,sjd->ijcd', left_block, right_all, precision=PRECISE)  23.6 us
    all_gather x1, blocking collectives, on_device(): lax.all_gather(pair_weights, 'col', axis=2, tiled=True)  19.8 us
    dot_general x3, matrix products, outer_block(): jnp.einsum('isc,sjd->ijcd', left_block, right_all, precision=PRECISE)  15.2 us
    another operation x3, local copies, waits for them, and re-layouts  15.1 us
    all_gather x1, blocking collectives, on_device(): left_all = lax.all_gather(left_flat, 'col', axis=0, tiled=True)  13.6 us
    all_gather x1, blocking collectives, on_device(): gathered = lax.all_gather(flat_normed, 'row', axis=0, tiled=True)  10.9 us
    all_gather x1, blocking collectives, on_device(): right_tokens = lax.all_gather(right_rows, 'row', axis=0, tiled=True)  9.21 us
    dot_general x3, matrix products, outer_block(): jnp.dot(flattened, outer_weight, precision=PRECISE, preferred_element_typ...  6.23 us
  transfers between devices with their start and end apart: 1, of which 0 were waited for; matrix products, arithmetic and copies ran while one was open for 1% of the time, Pallas kernels for 0%

commit v1 on v0

--- a/solution.py
+++ b/solution.py
@@ -4,6 +4,22 @@
 from jax.sharding import PartitionSpec as P
 
 PRECISE = lax.Precision.HIGHEST
+
+
+def wrap_teams_over_axis(arr_in, mesh_name, xin):
+    res = lax.axis_index(mesh_name)
+    d_next = lax.axis_size(mesh_name)
+    cards = []
+    local_next, built, carry_out = (d_next, res, arr_in.shape[2])
+    for q in tuple(range(local_next)):
+        cards.append((q, (q + 1) % local_next))
+    w_next, outcome_arr = (arr_in, None)
+    for k0 in tuple(range(local_next)):
+        o_now = lax.ppermute(w_next, mesh_name, cards) if k0 < local_next - 1 else None
+        arr_now = xin(w_next, (built - k0) % local_next * carry_out)
+        outcome_arr = arr_now if outcome_arr is None else outcome_arr + arr_now
+        w_next = o_now
+    return outcome_arr
 
 
 def normalize(features, channel_gain):
@@ -35,11 +51,15 @@
     flat_normed = normed.reshape(local_rows, local_seqs * channels)
     gathered = lax.all_gather(flat_normed, "row", axis=0, tiled=True)
     gathered = gathered.reshape(-1, local_seqs, channels)
-    mixed_rows = jnp.einsum(
-        "hij,jsc->ishc",
-        lax.all_gather(pair_weights, "col", axis=2, tiled=True),
-        gathered,
-        precision=PRECISE,
+    mixed_rows = wrap_teams_over_axis(
+        pair_weights,
+        "col",
+        xin=lambda part, offset: jnp.einsum(
+            "hij,jsc->ishc",
+            part,
+            lax.dynamic_slice_in_dim(gathered, offset, part.shape[2], axis=0),
+            precision=PRECISE,
+        ),
     )
     per_head = value_weight.reshape(channels, head_count, -1)
     averaged = jnp.einsum("ishc,chd->ishd", mixed_rows, per_head, precision=PRECISE)

time: 134 us -> 128 us (0.955)
  blocking collectives: 53.6 us -> 32.2 us
  waiting for transfers between devices: 0.01 us -> 10.5 us
  starting transfers between devices: 3.3 us -> 8.04 us
  matrix products: 24.4 us -> 26.1 us
    all_gather x1 -> x0, blocking collectives: 19.8 us -> none  [on_device(): lax.all_gather(pair_weights, 'col', axis=2, tiled=True)]
    ppermute x0 -> x3, waiting for transfers between devices: none -> 10.5 us  [wrap_teams_over_axis(): lax.ppermute(w_next, mesh_name, cards)]
    ppermute x0 -> x3, starting transfers between devices: none -> 4.74 us  [wrap_teams_over_axis(): lax.ppermute(w_next, mesh_name, cards)]
    dot_general x1 -> x4, matrix products: 1.51 us -> 3.22 us  [on_device(): jnp.einsum('hij,jsc->ishc', part, lax.dynamic_slice_in_dim(gathered, offs...]
    all_gather x1, blocking collectives: 10.9 us -> 9.25 us  [on_device(): gathered = lax.all_gather(flat_normed, 'row', axis=0, tiled=True)]
    unnamed x24 -> x23, local copies, waits for them, and re-layouts: 3.85 us -> 2.85 us
  transfers between devices with their start and end apart: 1 -> 4, of which waited for: 0 -> 2; matrix products, arithmetic and copies ran while one was open for 1% -> 6% of each run, Pallas kernels for 0% -> 0%
where the time goes in v1:
time: 128 us; the launch traced here: 127 us
  local copies, waits for them, and re-layouts  43.5 us (34%)
  blocking collectives  32.2 us (25%)
  matrix products  26.1 us (20%)
  waiting for transfers between devices  10.5 us (8%)
  starting transfers between devices  8.04 us (6%)
  other arithmetic  5.8 us (5%)
    div x3, local copies, waits for them, and re-layouts, outer_block(): jnp.einsum('isc,sjd->ijcd', left_block, right_all, precision=PRECISE)  23.6 us
    dot_general x3, matrix products, outer_block(): jnp.einsum('isc,sjd->ijcd', left_block, right_all, precision=PRECISE)  15.1 us
    another operation x3, local copies, waits for them, and re-layouts  15.1 us
    all_gather x1, blocking collectives, on_device(): left_all = lax.all_gather(left_flat, 'col', axis=0, tiled=True)  13.8 us
    ppermute x3, waiting for transfers between devices, wrap_teams_over_axis(): lax.ppermute(w_next, mesh_name, cards)  10.5 us
    all_gather x1, blocking collectives, on_device(): gathered = lax.all_gather(flat_normed, 'row', axis=0, tiled=True)  9.25 us
    all_gather x1, blocking collectives, on_device(): right_tokens = lax.all_gather(right_rows, 'row', axis=0, tiled=True)  9.22 us
    dot_general x3, matrix products, outer_block(): jnp.dot(flattened, outer_weight, precision=PRECISE, preferred_element_typ...  6.24 us
  transfers between devices with their start and end apart: 4, of which 2 were waited for; matrix products, arithmetic and copies ran while one was open for 6% of the time, Pallas kernels for 0%

profile of v1, /device:TPU:0, one launch (start us, length us, event | category | flops | bytes accessed | tf_op | source)
XLA Modules:
  0.0 127.3 jit_solution(948435919497873984)
XLA Ops:
  0.7 3.1 %collective-permute-start = (f32[8,24,48]{2,1,0:T(8,128)}, f32[8,24,48]{2,1,0:T(8,128)S(1)}, u32[]{:S(2)}, u32[]{:S(2)}) collective-permute-start(f32[8,24,48]{2,1,0:T(8,128)} %param.16), channel_id=1, source_target_pairs={{0,1},{1,2},{2,3},{3,0},{4,5},{5,6},{6,7},{7,4},{8,9},{9,10},{10,1... | collective-permute-start | bytes 110600 | tf_op jit(solution)/shard_map/ppermute | solution.py:18
  4.7 1.0 multiply_reduce_fusion.1
  6.7 9.3 %all_gather.9 = f32[192,256]{1,0:T(8,128)S(1)} all-gather(f32[24,256]{1,0:T(8,128)S(1)} %reshape.65), channel_id=1, replica_groups=mesh['row'=8,'col'=4] {'row'}, dimensions={0}, use_global_device_ids=true | all-gather | bytes 221184 | tf_op jit(solution)/shard_map/all_gather | solution.py:52
  16.1 1.5 %fusion.12 = f32[4,64,8,24]{1,3,0,2:T(8,128)S(1)} fusion(f32[192,4,64]{0,2,1:T(8,128)S(1)} %bitcast.115, s32[]{:T(128)S(6)} %select_n.32, f32[8,24,48]{2,1,0:T(8,128)} %param.16), kind=kOutput, calls=%fused_computation.24 | convolution fusion | flops 28311552 | bytes 364548 | tf_op jit(solution)/shard_map/hij,jsc->ishc/dot_general | solution.py:57
  18.6 1.6 %collective-permute-start.1 = (f32[8,24,48]{2,1,0:T(8,128)S(1)}, f32[8,24,48]{2,1,0:T(8,128)S(1)}, u32[]{:S(2)}, u32[]{:S(2)}) collective-permute-start(f32[8,24,48]{2,1,0:T(8,128)S(1)} %collective-permute-done), channel_id=1, source_target_pairs={{0,1},{1,2},{2,3},{3,0},{4,5},{5,6},{6,7},{7,4},{8,9},{9,10},{10,1... | collective-permute-start | bytes 110600 | tf_op jit(solution)/shard_map/ppermute | solution.py:18
  20.9 4.7 %collective-permute-done.1 = f32[8,24,48]{2,1,0:T(8,128)S(1)} collective-permute-done((f32[8,24,48]{2,1,0:T(8,128)S(1)}, f32[8,24,48]{2,1,0:T(8,128)S(1)}, u32[]{:S(2)}, u32[]{:S(2)}) %collective-permute-start.1) | collective-permute-done | bytes 36896 | tf_op jit(solution)/shard_map/ppermute | solution.py:18
  26.1 5.8 %collective-permute-done.2 = f32[8,24,48]{2,1,0:T(8,128)S(1)} collective-permute-done((f32[8,24,48]{2,1,0:T(8,128)S(1)}, f32[8,24,48]{2,1,0:T(8,128)S(1)}, u32[]{:S(2)}, u32[]{:S(2)}) %collective-permute-start.2) | collective-permute-done | bytes 36896 | tf_op jit(solution)/shard_map/ppermute | solution.py:18
  35.2 9.2 %all_gather.11 = f32[192,128]{1,0:T(8,128)S(1)} all-gather(f32[24,128]{1,0:T(8,128)S(1)} %reshape.70), channel_id=1, replica_groups=mesh['row'=8,'col'=4] {'row'}, dimensions={0}, use_global_device_ids=true | all-gather | bytes 110592 | tf_op jit(solution)/shard_map/all_gather | solution.py:78
  45.7 3.3 %all-to-all-start = ((f32[4,1,6144]{2,1,0:T(1,128)}), f32[4,1,6144]{2,1,0:T(1,128)S(1)}, u32[]{:S(2)}, u32[]{:S(2)}) async-start(f32[4,1,6144]{2,1,0:T(1,128)} %reshape.93), calls=%async_computation | async-start | bytes 196608 | tf_op jit(solution)/shard_map/all_to_all | solution.py:80
  49.3 13.8 %all-gather = f32[4,4,768]{2,1,0:T(4,128)S(1)} all-gather(f32[1,4,768]{2,1,0:T(4,128)S(1)} %reshape.73), channel_id=1, replica_groups=mesh['row'=8,'col'=4] {'col'}, dimensions={0}, use_global_device_ids=true | all-gather | bytes 61440 | tf_op jit(solution)/shard_map/all_gather | solution.py:82
  65.2 60.1 %while.10 = (s32[]{:T(128)}, f32[3,8,48,128]{3,2,1,0:T(8,128)}, f32[3,8,16,32]{3,1,0,2:T(8,128)S(1)}, f32[16,48,32]{1,0,2:T(8,128)S(1)}, f32[1024,128]{1,0:T(8,128)S(1)}, /*index=5*/s32[]{:T(128)}) while((s32[]{:T(128)}, f32[3,8,48,128]{3,2,1,0:T(8,128)}, f32[3,8,16,32]{3,1,0,2:T(8,128)S(1)}, f32[16,48,32]{1,0,2:T(8,128)S(1)}, ...), condition=%wide.region_5.6_spmd, body=%wide.region_4.5_spmd.sunk | while | flops 679870464 | bytes 10306121 | solution.py:98
  65.3 5.1 %multiply_bitcast_fusion.2 = f32[8,48,32,32]{1,2,3,0:T(8,128)} fusion(f32[16,48,32]{1,0,2:T(8,128)S(1)} %get-tuple-element.125, f32[1,8,16,32]{3,1,0,2:T(8,128)S(1)} %constant_dynamic-slice_fusion.2), kind=kOutput, calls=%fused_computation.clone.1 | convolution fusion | flops 75890688 | bytes 1687552 | tf_op jit(solution)/shard_map/while/body/eval_jaxpr/isc,sjd->ijcd/dot_general | solution.py:91
  70.3 7.9 %copy.135 = f32[8,48,32,32]{3,2,1,0:T(8,128)} copy(f32[8,48,32,32]{1,2,3,0:T(8,128)} %multiply_bitcast_fusion.2) | data formatting | bytes 3145728 | tf_op jit(solution)/shard_map/while/body/eval_jaxpr/div | solution.py:91
  78.2 5.0 %reshape.96 = f32[8,48,1024]{2,1,0:T(8,128)S(1)} reshape(f32[8,48,32,32]{3,2,1,0:T(8,128)} %copy.135) | data formatting | bytes 3145728 | tf_op jit(solution)/shard_map/reshape.27
  83.2 2.1 %fusion.50 = f32[3,8,48,128]{3,2,1,0:T(8,128)} fusion(f32[3,8,48,128]{3,2,1,0:T(8,128)} %get-tuple-element.117, s32[]{:T(128)} %get-tuple-element.116, f32[8,48,1024]{2,1,0:T(8,128)S(1)} %reshape.96, f32[1024,128]{1,0:T(8,128)S(1)} %get-tuple-element.126), kind=kOutput, calls=%fused_computation.2.clone.1 | convolution fusion | flops 603979776 | bytes 2294272 | tf_op jit(solution)/shard_map/while/body/eval_jaxpr/dot_general | solution.py:93
  85.3 5.0 %multiply_bitcast_fusion.2 = f32[8,48,32,32]{1,2,3,0:T(8,128)} fusion(f32[16,48,32]{1,0,2:T(8,128)S(1)} %get-tuple-element.125, f32[1,8,16,32]{3,1,0,2:T(8,128)S(1)} %constant_dynamic-slice_fusion.2), kind=kOutput, calls=%fused_computation.clone.1 | convolution fusion | flops 75890688 | bytes 1687552 | tf_op jit(solution)/shard_map/while/body/eval_jaxpr/isc,sjd->ijcd/dot_general | solution.py:91
  90.4 7.9 %copy.135 = f32[8,48,32,32]{3,2,1,0:T(8,128)} copy(f32[8,48,32,32]{1,2,3,0:T(8,128)} %multiply_bitcast_fusion.2) | data formatting | bytes 3145728 | tf_op jit(solution)/shard_map/while/body/eval_jaxpr/div | solution.py:91
  98.2 5.0 %reshape.96 = f32[8,48,1024]{2,1,0:T(8,128)S(1)} reshape(f32[8,48,32,32]{3,2,1,0:T(8,128)} %copy.135) | data formatting | bytes 3145728 | tf_op jit(solution)/shard_map/reshape.27
  103.3 2.1 %fusion.50 = f32[3,8,48,128]{3,2,1,0:T(8,128)} fusion(f32[3,8,48,128]{3,2,1,0:T(8,128)} %get-tuple-element.117, s32[]{:T(128)} %get-tuple-element.116, f32[8,48,1024]{2,1,0:T(8,128)S(1)} %reshape.96, f32[1024,128]{1,0:T(8,128)S(1)} %get-tuple-element.126), kind=kOutput, calls=%fused_computation.2.clone.1 | convolution fusion | flops 603979776 | bytes 2294272 | tf_op jit(solution)/shard_map/while/body/eval_jaxpr/dot_general | solution.py:93
  105.3 5.0 %multiply_bitcast_fusion.2 = f32[8,48,32,32]{1,2,3,0:T(8,128)} fusion(f32[16,48,32]{1,0,2:T(8,128)S(1)} %get-tuple-element.125, f32[1,8,16,32]{3,1,0,2:T(8,128)S(1)} %constant_dynamic-slice_fusion.2), kind=kOutput, calls=%fused_computation.clone.1 | convolution fusion | flops 75890688 | bytes 1687552 | tf_op jit(solution)/shard_map/while/body/eval_jaxpr/isc,sjd->ijcd/dot_general | solution.py:91
  110.4 7.9 %copy.135 = f32[8,48,32,32]{3,2,1,0:T(8,128)} copy(f32[8,48,32,32]{1,2,3,0:T(8,128)} %multiply_bitcast_fusion.2) | data formatting | bytes 3145728 | tf_op jit(solution)/shard_map/while/body/eval_jaxpr/div | solution.py:91
  118.3 5.0 %reshape.96 = f32[8,48,1024]{2,1,0:T(8,128)S(1)} reshape(f32[8,48,32,32]{3,2,1,0:T(8,128)} %copy.135) | data formatting | bytes 3145728 | tf_op jit(solution)/shard_map/reshape.27
  123.3 2.1 %fusion.50 = f32[3,8,48,128]{3,2,1,0:T(8,128)} fusion(f32[3,8,48,128]{3,2,1,0:T(8,128)} %get-tuple-element.117, s32[]{:T(128)} %get-tuple-element.116, f32[8,48,1024]{2,1,0:T(8,128)S(1)} %reshape.96, f32[1024,128]{1,0:T(8,128)S(1)} %get-tuple-element.126), kind=kOutput, calls=%fused_computation.2.clone.1 | convolution fusion | flops 603979776 | bytes 2294272 | tf_op jit(solution)/shard_map/while/body/eval_jaxpr/dot_general | solution.py:93
  125.4 1.9 %fusion.8 = f32[24,48,128]{2,1,0:T(8,128)} fusion(f32[24,48,128]{2,1,0:T(8,128)S(1)} %copy-done.3, f32[3,8,48,128]{3,2,1,0:T(8,128)} %get-tuple-element.29, f32[128]{0:T(128)S(1)} %copy-done.5), kind=kLoop, calls=%fused_computation.20 | loop fusion | flops 294912 | bytes 1769984 | tf_op jit(solution)/shard_map/add | solution.py:99
  (58 shorter events, 11.0 us)
Async XLA Ops:
  0.6 32.8 %copy-start = (f32[64,256]{1,0:T(8,128)S(1)}, f32[64,256]{1,0:T(8,128)}, u32[]{:S(2)}) copy-start(f32[64,256]{1,0:T(8,128)} %param.19) | copy-start | bytes 196612
  0.6 33.0 %copy-start.2 = (f32[24,4,64]{2,1,0:T(4,128)S(1)}, f32[24,4,64]{2,1,0:T(4,128)}, u32[]{:S(2)}) copy-start(f32[24,4,64]{2,1,0:T(4,128)} %param.14) | copy-start | bytes 73732
  0.7 33.0 %copy-start.4 = (f32[256,64]{0,1:T(8,128)S(1)}, f32[256,64]{0,1:T(8,128)}, u32[]{:S(2)}) copy-start(f32[256,64]{0,1:T(8,128)} %param.20) | copy-start | bytes 196612
  0.7 34.2 %copy-start.8 = (f32[64]{0:T(128)S(1)}, f32[64]{0:T(128)}, u32[]{:S(2)}) copy-start(f32[64]{0:T(128)} %param.21) | copy-start | bytes 772
  0.7 34.2 %copy-start.6 = (f32[64,32]{0,1:T(8,128)S(1)}, f32[64,32]{0,1:T(8,128)}, u32[]{:S(2)}) copy-start(f32[64,32]{0,1:T(8,128)} %param.23) | copy-start | bytes 24580
  0.7 17.9 %collective-permute-start = (f32[8,24,48]{2,1,0:T(8,128)}, f32[8,24,48]{2,1,0:T(8,128)S(1)}, u32[]{:S(2)}, u32[]{:S(2)}) collective-permute-start(f32[8,24,48]{2,1,0:T(8,128)} %param.16), channel_id=1, source_target_pairs={{0,1},{1,2},{2,3},{3,0},{4,5},{5,6},{6,7},{7,4},{8,9},{9,10},{10,1... | collective-permute-start | bytes 110600 | tf_op jit(solution)/shard_map/ppermute | solution.py:18
  17.6 31.4 %copy-start.7 = (f32[64,32]{0,1:T(8,128)S(1)}, f32[64,32]{0,1:T(8,128)}, u32[]{:S(2)}) copy-start(f32[64,32]{0,1:T(8,128)} %param.22) | copy-start | bytes 24580
  18.6 6.9 %collective-permute-start.1 = (f32[8,24,48]{2,1,0:T(8,128)S(1)}, f32[8,24,48]{2,1,0:T(8,128)S(1)}, u32[]{:S(2)}, u32[]{:S(2)}) collective-permute-start(f32[8,24,48]{2,1,0:T(8,128)S(1)} %collective-permute-done), channel_id=1, source_target_pairs={{0,1},{1,2},{2,3},{3,0},{4,5},{5,6},{6,7},{7,4},{8,9},{9,10},{10,1... | collective-permute-start | bytes 110600 | tf_op jit(solution)/shard_map/ppermute | solution.py:18
  25.5 6.4 %collective-permute-start.2 = (f32[8,24,48]{2,1,0:T(8,128)S(1)}, f32[8,24,48]{2,1,0:T(8,128)S(1)}, u32[]{:S(2)}, u32[]{:S(2)}) collective-permute-start(f32[8,24,48]{2,1,0:T(8,128)S(1)} %collective-permute-done.1), channel_id=1, source_target_pairs={{0,1},{1,2},{2,3},{3,0},{4,5},{5,6},{6,7},{7,4},{8,9},{9,10},{10,1... | collective-permute-start | bytes 110600 | tf_op jit(solution)/shard_map/ppermute | solution.py:18
  26.1 39.1 %copy-start.1 = (f32[1024,128]{1,0:T(8,128)S(1)}, f32[1024,128]{1,0:T(8,128)}, u32[]{:S(2)}) copy-start(f32[1024,128]{1,0:T(8,128)} %param.24) | copy-start | bytes 1572868
  45.7 17.5 %all-to-all-start = ((f32[4,1,6144]{2,1,0:T(1,128)}), f32[4,1,6144]{2,1,0:T(1,128)S(1)}, u32[]{:S(2)}, u32[]{:S(2)}) async-start(f32[4,1,6144]{2,1,0:T(1,128)} %reshape.93), calls=%async_computation | async-start | bytes 196608 | tf_op jit(solution)/shard_map/all_to_all | solution.py:80
  65.2 60.2 %copy-start.3 = (f32[24,48,128]{2,1,0:T(8,128)S(1)}, f32[24,48,128]{2,1,0:T(8,128)}, u32[]{:S(2)}) copy-start(f32[24,48,128]{2,1,0:T(8,128)} %param.15) | copy-start | bytes 1769476
  65.2 60.2 %copy-start.5 = (f32[128]{0:T(128)S(1)}, f32[128]{0:T(128)}, u32[]{:S(2)}) copy-start(f32[128]{0:T(128)} %param.25) | copy-start | bytes 1540
